TPU v7x, 32 devices: a whole 2x2x4 slice. The times are simulated.
32 devices in a mesh: dp: 8 (over y, x, core), ctx: 4 (over z).
Axes of the slice: x: 2, y: 2, z: 4, core: 2. Of those that a mesh axis runs over, the one named last changes fastest.
Arguments:
- activations: bfloat16 [8, 512, 2048], P('dp', 'ctx'), may hold values from -6 to 6
- segment_ids: int32 [8, 512], P('dp'), may hold values from 0 to 3, never falling along the last dimension, each value on 1 to 256 neighbouring positions
- ln1_gain: bfloat16 [2048], P(('dp', 'ctx')), may hold values from 0.25 to 1.75
- ln1_bias: bfloat16 [2048], P(('dp', 'ctx')), may hold values from -3 to 3
- q_weight: bfloat16 [2048, 2048], P(('dp', 'ctx')), may hold values from -0.125 to 0.125
- q_bias: bfloat16 [2048], P(('dp', 'ctx')), may hold values from -3 to 3
- kv_weight: bfloat16 [2048, 256], P(('dp', 'ctx')), may hold values from -0.125 to 0.125
- v_bias: bfloat16 [128], P(('dp', 'ctx')), may hold values from -3 to 3
- out_weight: bfloat16 [2048, 2048], P(('dp', 'ctx')), may hold values from -1 to 1
- out_bias: bfloat16 [2048], P(('dp', 'ctx')), may hold values from -3 to 3
- ln2_gain: bfloat16 [2048], P(('dp', 'ctx')), may hold values from 0.25 to 1.75
- ln2_bias: bfloat16 [2048], P(('dp', 'ctx')), may hold values from -3 to 3
- up_weight: bfloat16 [2048, 8192], P(('dp', 'ctx')), may hold values from -0.125 to 0.125
- up_bias: bfloat16 [8192], P(('dp', 'ctx')), may hold values from -3 to 3
- down_weight: bfloat16 [8192, 2048], P(('dp', 'ctx')), may hold values from -0.0625 to 0.0625
- down_bias: bfloat16 [2048], P(('dp', 'ctx')), may hold values from -3 to 3
- cotangent: bfloat16 [8, 512, 2048], P('dp', 'ctx'), may hold values from -6 to 6
Outputs:
- output: bfloat16 [8, 512, 2048], P('dp', 'ctx')
- input_grad: bfloat16 [8, 512, 2048], P('dp', 'ctx')
- ln1_gain_grad: float32 [2048], P(('dp', 'ctx'))
- ln1_bias_grad: float32 [2048], P(('dp', 'ctx'))
- q_weight_grad: float32 [2048, 2048], P(('dp', 'ctx'))
- q_bias_grad: float32 [2048], P(('dp', 'ctx'))
- kv_weight_grad: float32 [2048, 256], P(('dp', 'ctx'))
- v_bias_grad: float32 [128], P(('dp', 'ctx'))
- out_weight_grad: float32 [2048, 2048], P(('dp', 'ctx'))
- out_bias_grad: float32 [2048], P(('dp', 'ctx'))
- ln2_gain_grad: float32 [2048], P(('dp', 'ctx'))
- ln2_bias_grad: float32 [2048], P(('dp', 'ctx'))
- up_weight_grad: float32 [2048, 8192], P(('dp', 'ctx'))
- up_bias_grad: float32 [8192], P(('dp', 'ctx'))
- down_weight_grad: float32 [8192, 2048], P(('dp', 'ctx'))
- down_bias_grad: float32 [2048], P(('dp', 'ctx'))
Inputs may be any that keep to these rules, and one draw needn't show every extreme that they name: segment_ids of a row never fall; every one of the 4 documents of a row holds 1 to 256 tokens, and one holds exactly 256.
All inputs are finite; a program needn't handle non-finite values.
Results may differ from a plain program's by a relative error of at most 0.013.
Values may be sent and summed in bfloat16 or wider, within the bound.
No kernel may reach another device: no remote copies, remote signals or barrier semaphores. Data moves between devices by JAX's collectives and lax.ppermute only.
A program may use at most 320 MiB of HBM per device.

v0:
```python
import jax
import jax.numpy as jnp
from jax import lax
from jax.sharding import PartitionSpec as P

HEADS = 16
HD = 128
epsilon = 1e-05


def norm_rows(values, gain, shift):
    center = jnp.mean(values, axis=-1, keepdims=True)
    centered = values - center
    variance = jnp.mean(centered * centered, axis=-1, keepdims=True)
    return centered * lax.rsqrt(variance + epsilon) * gain + shift


def gelu_tanh(values):
    return jax.nn.gelu(values, approximate=True)


def local(
    activations,
    segment_ids,
    ln1_gain,
    ln1_bias,
    q_weight,
    q_bias,
    kv_weight,
    v_bias,
    out_weight,
    out_bias,
    ln2_gain,
    ln2_bias,
    up_weight,
    up_bias,
    down_weight,
    down_bias,
    cotangent,
):
    row_input = activations[0].astype(jnp.float32)
    tokens_here = row_input.shape[0]
    block_index = lax.axis_index("ctx")
    row_segments = segment_ids[0]
    attn_full = (
        lax.all_gather(ln1_gain, ("dp", "ctx"), axis=0, tiled=True),
        lax.all_gather(ln1_bias, ("dp", "ctx"), axis=0, tiled=True),
        lax.all_gather(q_weight, ("dp", "ctx"), axis=0, tiled=True),
        lax.all_gather(q_bias, ("dp", "ctx"), axis=0, tiled=True),
        lax.all_gather(kv_weight, ("dp", "ctx"), axis=0, tiled=True),
        lax.all_gather(v_bias, ("dp", "ctx"), axis=0, tiled=True),
        lax.all_gather(out_weight, ("dp", "ctx"), axis=0, tiled=True),
        lax.all_gather(out_bias, ("dp", "ctx"), axis=0, tiled=True),
    )
    gain_one, shift_one, weight_query, bias_query, weight_kv, bias_value, weight_out, bias_out = (
        attn_full
    )
    normed_one, norm_back_one = jax.vjp(
        norm_rows, row_input, gain_one.astype(jnp.float32), shift_one.astype(jnp.float32)
    )
    hidden_one = normed_one.astype(jnp.bfloat16)
    query_low = (
        jnp.dot(hidden_one, weight_query, preferred_element_type=jnp.float32)
        + bias_query.astype(jnp.float32)
    ).astype(jnp.bfloat16)
    kv_shift = jnp.concatenate([jnp.zeros((HD,), jnp.float32), bias_value.astype(jnp.float32)])
    kv_low = (jnp.dot(hidden_one, weight_kv, preferred_element_type=jnp.float32) + kv_shift).astype(
        jnp.bfloat16
    )
    kv_whole = lax.all_gather(kv_low, "ctx", axis=0, tiled=True)
    key_rows = kv_whole[:, :HD]
    value_rows = kv_whole[:, HD:]
    query_heads = query_low.reshape(tokens_here, HEADS, HD)
    scale_factor = HD ** (-0.5)
    query_start = block_index * tokens_here
    query_places = query_start + jnp.arange(tokens_here, dtype=jnp.int32)
    key_places = jnp.arange(kv_whole.shape[0], dtype=jnp.int32)
    query_segments = lax.dynamic_slice_in_dim(row_segments, query_start, tokens_here)
    allowed = (key_places[None, :] <= query_places[:, None]) & (
        row_segments[None, :] == query_segments[:, None]
    )

    def masked_scores():
        raw_scores = (
            jnp.einsum("thd,jd->htj", query_heads, key_rows, preferred_element_type=jnp.float32)
            * scale_factor
        )
        return jnp.where(allowed[None], raw_scores, -1e30)

    scores = masked_scores()
    biggest = jnp.max(scores, axis=-1, keepdims=True)
    expons = jnp.exp(scores - biggest)
    row_total = jnp.sum(expons, axis=-1, keepdims=True)
    log_total = biggest + jnp.log(row_total)
    soft_low = (expons / row_total).astype(jnp.bfloat16)
    attended = (
        jnp.einsum("htj,jd->thd", soft_low, value_rows, preferred_element_type=jnp.float32)
        .reshape(tokens_here, HEADS * HD)
        .astype(jnp.bfloat16)
    )
    middle = (
        row_input
        + jnp.dot(attended, weight_out, preferred_element_type=jnp.float32)
        + bias_out.astype(jnp.float32)
    )
    mlp_full = (
        lax.all_gather(ln2_gain, ("dp", "ctx"), axis=0, tiled=True),
        lax.all_gather(ln2_bias, ("dp", "ctx"), axis=0, tiled=True),
        lax.all_gather(up_weight, ("dp", "ctx"), axis=0, tiled=True),
        lax.all_gather(up_bias, ("dp", "ctx"), axis=0, tiled=True),
        lax.all_gather(down_weight, ("dp", "ctx"), axis=0, tiled=True),
        lax.all_gather(down_bias, ("dp", "ctx"), axis=0, tiled=True),
    )
    gain_two, shift_two, weight_up, bias_up, weight_down, bias_down = mlp_full
    normed_two, norm_back_two = jax.vjp(
        norm_rows, middle, gain_two.astype(jnp.float32), shift_two.astype(jnp.float32)
    )
    hidden_two = normed_two.astype(jnp.bfloat16)
    preact = jnp.dot(hidden_two, weight_up, preferred_element_type=jnp.float32) + bias_up.astype(
        jnp.float32
    )
    activ_full, gelu_back = jax.vjp(gelu_tanh, preact)
    activ = activ_full.astype(jnp.bfloat16)
    result = (
        middle
        + jnp.dot(activ, weight_down, preferred_element_type=jnp.float32)
        + bias_down.astype(jnp.float32)
    )
    mlp_back = (
        lax.all_gather(ln2_gain, ("dp", "ctx"), axis=0, tiled=True),
        lax.all_gather(ln2_bias, ("dp", "ctx"), axis=0, tiled=True),
        lax.all_gather(up_weight, ("dp", "ctx"), axis=0, tiled=True),
        lax.all_gather(up_bias, ("dp", "ctx"), axis=0, tiled=True),
        lax.all_gather(down_weight, ("dp", "ctx"), axis=0, tiled=True),
        lax.all_gather(down_bias, ("dp", "ctx"), axis=0, tiled=True),
    )
    weight_up_back = mlp_back[2]
    weight_down_back = mlp_back[4]
    grad_low = cotangent[0]
    grad_result = grad_low.astype(jnp.float32)
    grad_activ = jnp.einsum(
        "td,fd->tf", grad_low, weight_down_back, preferred_element_type=jnp.float32
    )
    grad_bias_down = jnp.sum(grad_result, axis=0)
    grad_weight_down = jnp.einsum("tf,td->fd", activ, grad_low, preferred_element_type=jnp.float32)
    down_sums = (
        lax.psum_scatter(grad_weight_down, ("dp", "ctx"), scatter_dimension=0, tiled=True),
        lax.psum_scatter(grad_bias_down, ("dp", "ctx"), scatter_dimension=0, tiled=True),
    )
    grad_preact = gelu_back(grad_activ)[0].astype(jnp.bfloat16)
    grad_bias_up = jnp.sum(grad_preact.astype(jnp.float32), axis=0)
    grad_hidden_two = jnp.einsum(
        "tf,df->td", grad_preact, weight_up_back, preferred_element_type=jnp.float32
    )
    grad_weight_up = jnp.einsum(
        "td,tf->df", hidden_two, grad_preact, preferred_element_type=jnp.float32
    )
    grad_mid_norm, grad_gain_two, grad_shift_two = norm_back_two(grad_hidden_two)
    grad_middle = grad_result + grad_mid_norm
    up_sums = (
        lax.psum_scatter(grad_gain_two, ("dp", "ctx"), scatter_dimension=0, tiled=True),
        lax.psum_scatter(grad_shift_two, ("dp", "ctx"), scatter_dimension=0, tiled=True),
        lax.psum_scatter(grad_weight_up, ("dp", "ctx"), scatter_dimension=0, tiled=True),
        lax.psum_scatter(grad_bias_up, ("dp", "ctx"), scatter_dimension=0, tiled=True),
    )
    attn_back = (
        lax.all_gather(ln1_gain, ("dp", "ctx"), axis=0, tiled=True),
        lax.all_gather(ln1_bias, ("dp", "ctx"), axis=0, tiled=True),
        lax.all_gather(q_weight, ("dp", "ctx"), axis=0, tiled=True),
        lax.all_gather(q_bias, ("dp", "ctx"), axis=0, tiled=True),
        lax.all_gather(kv_weight, ("dp", "ctx"), axis=0, tiled=True),
        lax.all_gather(v_bias, ("dp", "ctx"), axis=0, tiled=True),
        lax.all_gather(out_weight, ("dp", "ctx"), axis=0, tiled=True),
        lax.all_gather(out_bias, ("dp", "ctx"), axis=0, tiled=True),
    )
    weight_query_back = attn_back[2]
    weight_kv_back = attn_back[4]
    weight_out_back = attn_back[6]
    grad_branch = grad_middle.astype(jnp.bfloat16)
    grad_bias_out = jnp.sum(grad_branch.astype(jnp.float32), axis=0)
    grad_weight_out = jnp.einsum(
        "ti,td->id", attended, grad_branch, preferred_element_type=jnp.float32
    )
    grad_attended = (
        jnp.einsum("td,id->ti", grad_branch, weight_out_back, preferred_element_type=jnp.float32)
        .astype(jnp.bfloat16)
        .reshape(tokens_here, HEADS, HD)
    )
    soft_rows = jnp.exp(masked_scores() - log_total)
    soft_again = soft_rows.astype(jnp.bfloat16)
    grad_soft = jnp.einsum(
        "thd,jd->htj", grad_attended, value_rows, preferred_element_type=jnp.float32
    )
    inner_sum = jnp.sum(soft_rows * grad_soft, axis=-1, keepdims=True)
    grad_scores = (soft_rows * (grad_soft - inner_sum)).astype(jnp.bfloat16)
    grad_query = (
        (
            jnp.einsum("htj,jd->thd", grad_scores, key_rows, preferred_element_type=jnp.float32)
            * scale_factor
        )
        .astype(jnp.bfloat16)
        .reshape(tokens_here, HEADS * HD)
    )
    grad_keys = (
        jnp.einsum("htj,thd->jd", grad_scores, query_heads, preferred_element_type=jnp.float32)
        * scale_factor
    )
    grad_values = jnp.einsum(
        "htj,thd->jd", soft_again, grad_attended, preferred_element_type=jnp.float32
    )
    grad_kv_part = jnp.concatenate([grad_keys, grad_values], axis=1)
    grad_kv = lax.psum_scatter(
        grad_kv_part.astype(jnp.bfloat16), "ctx", scatter_dimension=0, tiled=True
    )
    grad_bias_query = jnp.sum(grad_query.astype(jnp.float32), axis=0)
    grad_weight_query = jnp.einsum(
        "td,te->de", hidden_one, grad_query, preferred_element_type=jnp.float32
    )
    grad_bias_value = jnp.sum(grad_kv[:, HD:].astype(jnp.float32), axis=0)
    grad_weight_kv = jnp.einsum(
        "td,te->de", hidden_one, grad_kv, preferred_element_type=jnp.float32
    )
    grad_hidden_one = jnp.einsum(
        "te,de->td", grad_query, weight_query_back, preferred_element_type=jnp.float32
    ) + jnp.einsum("te,de->td", grad_kv, weight_kv_back, preferred_element_type=jnp.float32)
    grad_row_norm, grad_gain_one, grad_shift_one = norm_back_one(grad_hidden_one)
    grad_input = grad_middle + grad_row_norm
    attn_sums = (
        lax.psum_scatter(grad_gain_one, ("dp", "ctx"), scatter_dimension=0, tiled=True),
        lax.psum_scatter(grad_shift_one, ("dp", "ctx"), scatter_dimension=0, tiled=True),
        lax.psum_scatter(grad_weight_query, ("dp", "ctx"), scatter_dimension=0, tiled=True),
        lax.psum_scatter(grad_bias_query, ("dp", "ctx"), scatter_dimension=0, tiled=True),
        lax.psum_scatter(grad_weight_kv, ("dp", "ctx"), scatter_dimension=0, tiled=True),
        lax.psum_scatter(grad_bias_value, ("dp", "ctx"), scatter_dimension=0, tiled=True),
        lax.psum_scatter(grad_weight_out, ("dp", "ctx"), scatter_dimension=0, tiled=True),
        lax.psum_scatter(grad_bias_out, ("dp", "ctx"), scatter_dimension=0, tiled=True),
    )
    return (
        result.astype(jnp.bfloat16)[None],
        grad_input.astype(jnp.bfloat16)[None],
        attn_sums[0],
        attn_sums[1],
        attn_sums[2],
        attn_sums[3],
        attn_sums[4],
        attn_sums[5],
        attn_sums[6],
        attn_sums[7],
        up_sums[0],
        up_sums[1],
        up_sums[2],
        up_sums[3],
        down_sums[0],
        down_sums[1],
    )


def solution(mesh):
    in_specs = (
        P("dp", "ctx", None),
        P("dp", None),
        P(("dp", "ctx")),
        P(("dp", "ctx")),
        P(("dp", "ctx"), None),
        P(("dp", "ctx")),
        P(("dp", "ctx"), None),
        P(("dp", "ctx")),
        P(("dp", "ctx"), None),
        P(("dp", "ctx")),
        P(("dp", "ctx")),
        P(("dp", "ctx")),
        P(("dp", "ctx"), None),
        P(("dp", "ctx")),
        P(("dp", "ctx"), None),
        P(("dp", "ctx")),
        P("dp", "ctx", None),
    )
    out_specs = (
        P("dp", "ctx", None),
        P("dp", "ctx", None),
        P(("dp", "ctx")),
        P(("dp", "ctx")),
        P(("dp", "ctx"), None),
        P(("dp", "ctx")),
        P(("dp", "ctx"), None),
        P(("dp", "ctx")),
        P(("dp", "ctx"), None),
        P(("dp", "ctx")),
        P(("dp", "ctx")),
        P(("dp", "ctx")),
        P(("dp", "ctx"), None),
        P(("dp", "ctx")),
        P(("dp", "ctx"), None),
        P(("dp", "ctx")),
    )
    return jax.shard_map(local, mesh=mesh, in_specs=in_specs, out_specs=out_specs, check_vma=False)
```

profile of v0, /device:TPU:0, one launch (start us, length us, event | category | flops | bytes accessed | tf_op | source)
XLA Modules:
  0.0 4536.4 jit_solution(195619505325914754)
XLA Ops:
  17.4 42.8 all-reduce.19
  60.9 66.4 %all-gather = bf16[32,1,256]{2,1,0:T(2,128)(2,1)S(1)} all-gather(bf16[1,1,256]{2,1,0:T(2,128)(2,1)S(1)} %reshape.225), channel_id=1, replica_groups=mesh['dp'=8,'ctx'=4] {'dp','ctx'}, dimensions={0}, use_global_device_ids=true | all-gather | bytes 16896 | tf_op jit(solution)/shard_map/all_gather | solution.py:110
  131.5 1.8 fusion.38
  133.3 16.1 all_gather.54
  149.4 4.7 fusion.14
  158.2 70.7 %all-gather.11.cloned.1.call-done = bf16[2048,2048]{1,0:T(8,128)(2,1)} async-done(((bf16[64,2048]{1,0:T(8,128)(2,1)}), bf16[2048,2048]{1,0:T(8,128)(2,1)}) %all-gather.11.cloned.1.call-update) | async-done | bytes 8388624 | tf_op jit(solution)/shard_map/all_gather | solution.py:52
  228.9 4.7 fusion.77
  233.9 191.2 %all-gather.13.cloned.1.call-done = bf16[2048,8192]{1,0:T(8,128)(2,1)} async-done(((bf16[64,8192]{1,0:T(8,128)(2,1)}), bf16[2048,8192]{1,0:T(8,128)(2,1)}) %all-gather.13.cloned.1.call-update) | async-done | bytes 33554448 | tf_op jit(solution)/shard_map/all_gather | solution.py:109
  425.1 18.0 convolution_add_fusion
  443.1 177.8 %all-gather.15.cloned.1.call-done = bf16[8192,2048]{1,0:T(8,128)(2,1)} async-done(((bf16[256,2048]{1,0:T(8,128)(2,1)}), bf16[8192,2048]{1,0:T(8,128)(2,1)}) %all-gather.15.cloned.1.call-update) | async-done | bytes 33554448 | tf_op jit(solution)/shard_map/all_gather | solution.py:111
  620.8 20.1 convert_reduce_fusion
  641.0 19.8 multiply_reduce_fusion
  664.0 7.1 convolution_convert_fusion
  671.1 2.0 copy.65
  673.2 3.3 fusion.7
  678.6 1.9 convert_reduce_fusion.4
  682.3 7.5 fusion.78
  689.7 10.5 reduce-scatter.19.cloned.1.call-done
  700.2 2.8 fusion.73
  704.1 2.0 convert_reduce_fusion.2
  706.9 1.9 fusion.69
  709.1 8.2 fusion.51
  718.5 8.0 fusion.79
  726.6 24.9 fusion.68
  751.9 25.5 fusion.53
  778.0 17.7 fusion.16
  795.8 36.1 all-reduce.22.cloned.1.call-done
  843.2 130.9 %reduce-scatter.11.cloned.1.call-done = f32[64,256]{1,0:T(8,128)} async-done(((f32[2048,256]{1,0:T(8,128)}), f32[64,256]{1,0:T(8,128)}) %reduce-scatter.11.cloned.1.call-update) | async-done | bytes 65552 | tf_op jit(solution)/shard_map/reduce_scatter | solution.py:233
  974.2 364.9 %reduce-scatter.9.cloned.1.call-done = f32[64,2048]{1,0:T(8,128)} async-done(((f32[2048,2048]{1,0:T(8,128)}), f32[64,2048]{1,0:T(8,128)}) %reduce-scatter.9.cloned.1.call-update) | async-done | bytes 524304 | tf_op jit(solution)/shard_map/reduce_scatter | solution.py:231
  1339.1 365.0 %reduce-scatter.13.cloned.1.call-done = f32[64,2048]{1,0:T(8,128)} async-done(((f32[2048,2048]{1,0:T(8,128)}), f32[64,2048]{1,0:T(8,128)}) %reduce-scatter.13.cloned.1.call-update) | async-done | bytes 524304 | tf_op jit(solution)/shard_map/reduce_scatter | solution.py:235
  1704.1 1411.7 %reduce-scatter.15.cloned.1.call-done = f32[64,8192]{1,0:T(8,128)} async-done(((f32[2048,8192]{1,0:T(8,128)}), f32[64,8192]{1,0:T(8,128)}) %reduce-scatter.15.cloned.1.call-update) | async-done | bytes 2097168 | tf_op jit(solution)/shard_map/reduce_scatter | solution.py:163
  3115.8 1413.5 %reduce-scatter.17.cloned.1.call-done = f32[256,2048]{1,0:T(8,128)} async-done(((f32[8192,2048]{1,0:T(8,128)}), f32[256,2048]{1,0:T(8,128)}) %reduce-scatter.17.cloned.1.call-update) | async-done | bytes 2097168 | tf_op jit(solution)/shard_map/reduce_scatter | solution.py:147
  (120 shorter events, 42.0 us)
Async XLA Ops:
  7.2 142.2 %copy-start.2 = (bf16[1,128,2048]{2,1,0:T(8,128)(2,1)S(1)}, bf16[1,128,2048]{2,1,0:T(8,128)(2,1)}, u32[]{:S(2)}) copy-start(bf16[1,128,2048]{2,1,0:T(8,128)(2,1)} %param.17) | copy-start | bytes 1572868
  7.2 124.3 %all-gather.7.cloned.1.call-start = ((), (), s32[]{:S(2)}) async-start(), calls=%async_computation.6 | async-start | bytes 1081344 | tf_op jit(solution)/shard_map/all_gather | solution.py:50
  7.9 141.5 %all-gather.9.cloned.1.call-start = ((), (), s32[]{:S(2)}) async-start(), calls=%async_computation.7 | async-start | bytes 8650752 | tf_op jit(solution)/shard_map/all_gather | solution.py:48
  8.7 220.2 %all-gather.11.cloned.1.call-start = ((), (), s32[]{:S(2)}) async-start(), calls=%async_computation.8 | async-start | bytes 8650752 | tf_op jit(solution)/shard_map/all_gather | solution.py:52
  9.4 415.7 %all-gather.13.cloned.1.call-start = ((), (), s32[]{:S(2)}) async-start(), calls=%async_computation.9 | async-start | bytes 34603008 | tf_op jit(solution)/shard_map/all_gather | solution.py:109
  10.0 610.9 %all-gather.15.cloned.1.call-start = ((), (), s32[]{:S(2)}) async-start(), calls=%async_computation.10 | async-start | bytes 34603008 | tf_op jit(solution)/shard_map/all_gather | solution.py:111
  10.6 689.7 %reduce-scatter.19.cloned.1.call-start = ((), (), s32[]{:S(2)}) async-start(), calls=%async_computation.16 | async-start | bytes 327680
  154.4 1.4 copy-start.10
  155.2 2.0 copy-start
  158.2 75.4 %copy-start.8 = (bf16[128,16,128]{2,0,1:T(8,128)(2,1)}, bf16[128,16,128]{2,0,1:T(8,128)(2,1)S(1)}, u32[]{:S(2)}) copy-start(bf16[128,16,128]{2,0,1:T(8,128)(2,1)S(1)} %fusion.27) | copy-start | bytes 1572868
  425.1 195.8 %copy-start.3 = (bf16[1,128,2048]{2,1,0:T(8,128)(2,1)S(1)}, bf16[1,128,2048]{2,1,0:T(8,128)(2,1)}, u32[]{:S(2)}) copy-start(bf16[1,128,2048]{2,1,0:T(8,128)(2,1)} %param.33) | copy-start | bytes 1572868
  663.2 0.8 copy-start.4
  673.1 3.6 copy-start.1
  673.2 3.7 copy-start.6
  677.7 2.8 copy-start.11
  682.2 149.7 %all-reduce.22.cloned.1.call-start = ((), (), s32[]{:S(2)}) async-start(), calls=%async_computation.17 | async-start | bytes 181248
  700.2 5.9 slice-start
  700.2 6.7 copy-start.12
  706.1 3.1 copy-start.7
  706.9 267.3 %reduce-scatter.11.cloned.1.call-start = ((), (), s32[]{:S(2)}) async-start(), calls=%async_computation.12 | async-start | bytes 2162688 | tf_op jit(solution)/shard_map/reduce_scatter | solution.py:233
  708.9 630.2 %reduce-scatter.9.cloned.1.call-start = ((), (), s32[]{:S(2)}) async-start(), calls=%async_computation.11 | async-start | bytes 17301504 | tf_op jit(solution)/shard_map/reduce_scatter | solution.py:231
  717.3 1.0 copy-start.5
  717.3 1.2 copy-start.9
  717.3 986.7 %reduce-scatter.13.cloned.1.call-start = ((), (), s32[]{:S(2)}) async-start(), calls=%async_computation.13 | async-start | bytes 17301504 | tf_op jit(solution)/shard_map/reduce_scatter | solution.py:235
  726.6 2389.2 %reduce-scatter.15.cloned.1.call-start = ((), (), s32[]{:S(2)}) async-start(), calls=%async_computation.14 | async-start | bytes 69206016 | tf_op jit(solution)/shard_map/reduce_scatter | solution.py:163
  751.6 3777.7 %reduce-scatter.17.cloned.1.call-start = ((), (), s32[]{:S(2)}) async-start(), calls=%async_computation.15 | async-start | bytes 69206016 | tf_op jit(solution)/shard_map/reduce_scatter | solution.py:147
  777.4 0.7 copy-start.13
Sparse Core Ops, SparseCore 0:
  11.0 56.6 all-gather.6
  70.7 78.4 all-gather.8
  152.1 76.7 all-gather.10
  231.6 193.3 all-gather.12
  427.8 192.9 all-gather.14
  682.3 17.8 reduce-scatter.18
  708.4 123.4 all-reduce.21
  834.7 139.4 reduce-scatter.10
  977.2 361.8 reduce-scatter.8
  1341.9 362.1 reduce-scatter.12
  1707.1 1408.5 reduce-scatter.14
  3118.7 1410.5 reduce-scatter.16
where the time goes:
time: 4540 us
  waiting for transfers between devices  4180 us (92%)
  matrix products  181 us (4%)
  blocking collectives  125 us (3%)
    reduce_scatter x1, waiting for transfers between devices, local(): lax.psum_scatter(grad_weight_down, ('dp', 'ctx'), scatter_dimension=0, ti...  1410 us
    reduce_scatter x1, waiting for transfers between devices, local(): lax.psum_scatter(grad_weight_up, ('dp', 'ctx'), scatter_dimension=0, tile...  1410 us
    reduce_scatter x1, waiting for transfers between devices, local(): lax.psum_scatter(grad_weight_out, ('dp', 'ctx'), scatter_dimension=0, til...  365 us
    reduce_scatter x1, waiting for transfers between devices, local(): lax.psum_scatter(grad_weight_query, ('dp', 'ctx'), scatter_dimension=0, t...  365 us
    all_gather x1, waiting for transfers between devices, local(): lax.all_gather(up_weight, ('dp', 'ctx'), axis=0, tiled=True)  191 us
    all_gather x1, waiting for transfers between devices, local(): lax.all_gather(down_weight, ('dp', 'ctx'), axis=0, tiled=True)  178 us
    reduce_scatter x1, waiting for transfers between devices, local(): lax.psum_scatter(grad_weight_kv, ('dp', 'ctx'), scatter_dimension=0, tile...  131 us
  transfers between devices with their start and end apart: 12, of which 10 were waited for; matrix products, arithmetic and copies ran while one was open for 3% of the time, Pallas kernels for 0%

commit v1 on v0

--- a/solution.py
+++ b/solution.py
@@ -38,6 +38,27 @@
     down_bias,
     cotangent,
 ):
+
+    def perform_frame_for(here_x, which_axis):
+        answer = jax.lax.axis_index(which_axis)
+        reached = jax.lax.axis_size(which_axis)
+        right_arr, state_now, current_value = (reached, answer, here_x.shape[0])
+        e_now, outer = (here_x, 1)
+        while outer < right_arr:
+            e_now = jnp.concatenate(
+                [
+                    e_now,
+                    jax.lax.ppermute(
+                        e_now,
+                        which_axis,
+                        [(idx, (idx - outer) % right_arr) for idx in range(right_arr)],
+                    ),
+                ],
+                axis=0,
+            )
+            outer = 2 * outer
+        return jnp.roll(e_now, shift=state_now * current_value, axis=0)
+
     row_input = activations[0].astype(jnp.float32)
     tokens_here = row_input.shape[0]
     block_index = lax.axis_index("ctx")
@@ -108,7 +129,7 @@
         lax.all_gather(ln2_bias, ("dp", "ctx"), axis=0, tiled=True),
         lax.all_gather(up_weight, ("dp", "ctx"), axis=0, tiled=True),
         lax.all_gather(up_bias, ("dp", "ctx"), axis=0, tiled=True),
-        lax.all_gather(down_weight, ("dp", "ctx"), axis=0, tiled=True),
+        perform_frame_for(down_weight, ("dp", "ctx")),
         lax.all_gather(down_bias, ("dp", "ctx"), axis=0, tiled=True),
     )
     gain_two, shift_two, weight_up, bias_up, weight_down, bias_down = mlp_full

time: 4540 us -> 4610 us (1.015)
  local copies, waits for them, and re-layouts: 27.1 us -> 89 us
    ppermute x0 -> x5, waiting for transfers between devices: none -> 855 us  [perform_frame_for(): jax.lax.ppermute(e_now, which_axis, [(idx, (idx - outer) % right_arr) for...]
    reduce_scatter x1, waiting for transfers between devices: 365 us -> 0.01 us  [local(): lax.psum_scatter(grad_weight_query, ('dp', 'ctx'), scatter_dimension=0, t...]
    reduce_scatter x1, waiting for transfers between devices: 365 us -> 41.9 us  [local(): lax.psum_scatter(grad_weight_out, ('dp', 'ctx'), scatter_dimension=0, til...]
    reduce_scatter x1, waiting for transfers between devices: 131 us -> 0.01 us  [local(): lax.psum_scatter(grad_weight_kv, ('dp', 'ctx'), scatter_dimension=0, tile...]
  transfers between devices with their start and end apart: 12 -> 17, of which waited for: 10 -> 12; matrix products, arithmetic and copies ran while one was open for 3% -> 5% of each run, Pallas kernels for 0% -> 0%
where the time goes in v1:
time: 4610 us; the launch traced here: 4600 us
  waiting for transfers between devices  4180 us (91%)
  matrix products  179 us (4%)
  blocking collectives  125 us (3%)
  local copies, waits for them, and re-layouts  89 us (2%)
    reduce_scatter x1, waiting for transfers between devices, local(): lax.psum_scatter(grad_weight_down, ('dp', 'ctx'), scatter_dimension=0, ti...  1410 us
    reduce_scatter x1, waiting for transfers between devices, local(): lax.psum_scatter(grad_weight_up, ('dp', 'ctx'), scatter_dimension=0, tile...  1410 us
    ppermute x5, waiting for transfers between devices, perform_frame_for(): jax.lax.ppermute(e_now, which_axis, [(idx, (idx - outer) % right_arr) for...  855 us
    all_gather x1, waiting for transfers between devices, local(): lax.all_gather(up_weight, ('dp', 'ctx'), axis=0, tiled=True)  191 us
    all_gather x1, waiting for transfers between devices, local(): lax.all_gather(down_weight, ('dp', 'ctx'), axis=0, tiled=True)  178 us
  transfers between devices with their start and end apart: 17, of which 12 were waited for; matrix products, arithmetic and copies ran while one was open for 5% of the time, Pallas kernels for 0%

profile of v1, /device:TPU:0, one launch (start us, length us, event | category | flops | bytes accessed | tf_op | source)
XLA Modules:
  0.0 4604.5 jit_solution(2856173056942458078)
XLA Ops:
  17.4 42.8 all-reduce.19
  60.9 66.4 %all-gather = bf16[32,1,256]{2,1,0:T(2,128)(2,1)S(1)} all-gather(bf16[1,1,256]{2,1,0:T(2,128)(2,1)S(1)} %reshape.225), channel_id=1, replica_groups=mesh['dp'=8,'ctx'=4] {'dp','ctx'}, dimensions={0}, use_global_device_ids=true | all-gather | bytes 16896 | tf_op jit(solution)/shard_map/all_gather | solution.py:131
  133.3 16.1 all_gather.53
  149.4 4.7 fusion.24
  158.0 70.8 %all-gather.11.cloned.1.call-done = bf16[2048,2048]{1,0:T(8,128)(2,1)} async-done(((bf16[64,2048]{1,0:T(8,128)(2,1)}), bf16[2048,2048]{1,0:T(8,128)(2,1)}) %all-gather.11.cloned.1.call-update) | async-done | bytes 8388624 | tf_op jit(solution)/shard_map/all_gather | solution.py:73
  228.8 4.7 fusion.89
  233.9 191.2 %all-gather.13.cloned.1.call-done = bf16[2048,8192]{1,0:T(8,128)(2,1)} async-done(((bf16[64,8192]{1,0:T(8,128)(2,1)}), bf16[2048,8192]{1,0:T(8,128)(2,1)}) %all-gather.13.cloned.1.call-update) | async-done | bytes 33554448 | tf_op jit(solution)/shard_map/all_gather | solution.py:130
  425.0 18.0 convolution_add_fusion
  443.0 177.8 %all-gather.15.cloned.1.call-done = bf16[8192,2048]{1,0:T(8,128)(2,1)} async-done(((bf16[256,2048]{1,0:T(8,128)(2,1)}), bf16[8192,2048]{1,0:T(8,128)(2,1)}) %all-gather.15.cloned.1.call-update) | async-done | bytes 33554448 | tf_op jit(solution)/shard_map/all_gather | solution.py:155
  620.8 19.7 convert_reduce_fusion
  640.5 19.8 multiply_reduce_fusion
  663.7 7.1 convolution_convert_fusion
  682.1 7.5 fusion.90
  689.5 10.5 reduce-scatter.19.cloned.1.call-done
  709.0 8.3 fusion.62
  718.5 8.1 fusion.91
  726.6 24.9 fusion.80
  751.6 25.5 fusion.64
  778.6 23.6 collective-permute-done
  802.5 96.2 %collective-permute-done.1 = bf16[512,2048]{1,0:T(8,128)(2,1)S(1)} collective-permute-done((bf16[512,2048]{1,0:T(8,128)(2,1)S(1)}, bf16[512,2048]{1,0:T(8,128)(2,1)S(1)}, u32[]{:S(2)}, u32[]{:S(2)}) %collective-permute-start.1) | collective-permute-done | bytes 2097184 | tf_op jit(solution)/shard_map/ppermute | solution.py:51
  900.7 49.9 %collective-permute-done.2 = bf16[1024,2048]{1,0:T(8,128)(2,1)S(1)} collective-permute-done((bf16[1024,2048]{1,0:T(8,128)(2,1)S(1)}, bf16[1024,2048]{1,0:T(8,128)(2,1)S(1)}, u32[]{:S(2)}, u32[]{:S(2)}) %collective-permute-start.2) | collective-permute-done | bytes 4194336 | tf_op jit(solution)/shard_map/ppermute | solution.py:51
  950.6 4.5 pad_maximum_fusion
  966.4 209.4 %collective-permute-done.3 = bf16[2048,2048]{1,0:T(8,128)(2,1)S(1)} collective-permute-done((bf16[2048,2048]{1,0:T(8,128)(2,1)}, bf16[2048,2048]{1,0:T(8,128)(2,1)S(1)}, u32[]{:S(2)}, u32[]{:S(2)}) %collective-permute-start.3) | collective-permute-done | bytes 8388640 | tf_op jit(solution)/shard_map/ppermute | solution.py:51
  1175.8 7.2 constant_dynamic-update-slice_fusion
  1184.1 476.1 %collective-permute-done.4 = bf16[4096,2048]{1,0:T(8,128)(2,1)} collective-permute-done((bf16[4096,2048]{1,0:T(8,128)(2,1)}, bf16[4096,2048]{1,0:T(8,128)(2,1)}, u32[]{:S(2)}, u32[]{:S(2)}) %collective-permute-start.4) | collective-permute-done | bytes 16777248 | tf_op jit(solution)/shard_map/ppermute | solution.py:51
  1660.2 14.5 constant_dynamic-update-slice_fusion.11
  1680.7 8.3 constant_dynamic-update-slice_fusion.6
  1688.9 14.2 constant_dynamic-update-slice_fusion.5
  1703.1 15.7 fusion.25
  1730.1 41.9 reduce-scatter.13.cloned.1.call-done
  1772.0 1411.6 %reduce-scatter.15.cloned.1.call-done = f32[64,8192]{1,0:T(8,128)} async-done(((f32[2048,8192]{1,0:T(8,128)}), f32[64,8192]{1,0:T(8,128)}) %reduce-scatter.15.cloned.1.call-update) | async-done | bytes 2097168 | tf_op jit(solution)/shard_map/reduce_scatter | solution.py:184
  3183.6 1413.5 %reduce-scatter.17.cloned.1.call-done = f32[256,2048]{1,0:T(8,128)} async-done(((f32[8192,2048]{1,0:T(8,128)}), f32[256,2048]{1,0:T(8,128)}) %reduce-scatter.17.cloned.1.call-update) | async-done | bytes 2097168 | tf_op jit(solution)/shard_map/reduce_scatter | solution.py:168
  (161 shorter events, 78.9 us)
Async XLA Ops:
  7.2 142.2 %copy-start.5 = (bf16[1,128,2048]{2,1,0:T(8,128)(2,1)S(1)}, bf16[1,128,2048]{2,1,0:T(8,128)(2,1)}, u32[]{:S(2)}) copy-start(bf16[1,128,2048]{2,1,0:T(8,128)(2,1)} %param.17) | copy-start | bytes 1572868
  7.2 124.2 %all-gather.7.cloned.1.call-start = ((), (), s32[]{:S(2)}) async-start(), calls=%async_computation.6 | async-start | bytes 1081344 | tf_op jit(solution)/shard_map/all_gather | solution.py:71
  7.9 141.4 %all-gather.9.cloned.1.call-start = ((), (), s32[]{:S(2)}) async-start(), calls=%async_computation.7 | async-start | bytes 8650752 | tf_op jit(solution)/shard_map/all_gather | solution.py:69
  8.7 220.2 %all-gather.11.cloned.1.call-start = ((), (), s32[]{:S(2)}) async-start(), calls=%async_computation.8 | async-start | bytes 8650752 | tf_op jit(solution)/shard_map/all_gather | solution.py:73
  9.4 415.6 %all-gather.13.cloned.1.call-start = ((), (), s32[]{:S(2)}) async-start(), calls=%async_computation.9 | async-start | bytes 34603008 | tf_op jit(solution)/shard_map/all_gather | solution.py:130
  10.0 610.8 %all-gather.15.cloned.1.call-start = ((), (), s32[]{:S(2)}) async-start(), calls=%async_computation.10 | async-start | bytes 34603008 | tf_op jit(solution)/shard_map/all_gather | solution.py:155
  10.6 689.5 %reduce-scatter.19.cloned.1.call-start = ((), (), s32[]{:S(2)}) async-start(), calls=%async_computation.16 | async-start | bytes 327680
  158.0 75.6 %copy-start.16 = (bf16[128,16,128]{2,0,1:T(8,128)(2,1)}, bf16[128,16,128]{2,0,1:T(8,128)(2,1)S(1)}, u32[]{:S(2)}) copy-start(bf16[128,16,128]{2,0,1:T(8,128)(2,1)S(1)} %fusion.38) | copy-start | bytes 1572868
  425.0 195.8 %copy-start.11 = (bf16[1,128,2048]{2,1,0:T(8,128)(2,1)S(1)}, bf16[1,128,2048]{2,1,0:T(8,128)(2,1)}, u32[]{:S(2)}) copy-start(bf16[1,128,2048]{2,1,0:T(8,128)(2,1)} %param.33) | copy-start | bytes 1572868
  672.8 3.6 copy-start.1
  672.8 3.7 copy-start.14
  682.0 1036.7 %all-reduce.22.cloned.1.call-start = ((), (), s32[]{:S(2)}) async-start(), calls=%async_computation.17 | async-start | bytes 181248
  700.0 5.9 slice-start
  700.0 6.7 copy-start.20
  706.7 1023.5 %reduce-scatter.11.cloned.1.call-start = ((), (), s32[]{:S(2)}) async-start(), calls=%async_computation.12 | async-start | bytes 2162688 | tf_op jit(solution)/shard_map/reduce_scatter | solution.py:254
  708.7 1021.5 %reduce-scatter.9.cloned.1.call-start = ((), (), s32[]{:S(2)}) async-start(), calls=%async_computation.11 | async-start | bytes 17301504 | tf_op jit(solution)/shard_map/reduce_scatter | solution.py:252
  717.3 1054.7 %reduce-scatter.13.cloned.1.call-start = ((), (), s32[]{:S(2)}) async-start(), calls=%async_computation.13 | async-start | bytes 17301504 | tf_op jit(solution)/shard_map/reduce_scatter | solution.py:256
  726.6 2457.0 %reduce-scatter.15.cloned.1.call-start = ((), (), s32[]{:S(2)}) async-start(), calls=%async_computation.14 | async-start | bytes 69206016 | tf_op jit(solution)/shard_map/reduce_scatter | solution.py:184
  751.6 3845.6 %reduce-scatter.17.cloned.1.call-start = ((), (), s32[]{:S(2)}) async-start(), calls=%async_computation.15 | async-start | bytes 69206016 | tf_op jit(solution)/shard_map/reduce_scatter | solution.py:168
  778.4 23.8 collective-permute-start
  802.2 155.8 %copy-start.9 = (bf16[256,2048]{1,0:T(8,128)(2,1)}, bf16[256,2048]{1,0:T(8,128)(2,1)S(1)}, u32[]{:S(2)}) copy-start(bf16[256,2048]{1,0:T(8,128)(2,1)S(1)} %collective-permute-done) | copy-start | bytes 3145732
  802.4 96.3 %collective-permute-start.1 = (bf16[512,2048]{1,0:T(8,128)(2,1)S(1)}, bf16[512,2048]{1,0:T(8,128)(2,1)S(1)}, u32[]{:S(2)}, u32[]{:S(2)}) collective-permute-start(bf16[512,2048]{1,0:T(8,128)(2,1)S(1)} %pad_maximum_fusion.2), channel_id=1, source_target_pairs={{0,30},{1,31},{2,0},{3,1},{4,2},{5,3},{6,4},{7,5},{8,6},{9,7},{10,... | collective-permute-start | bytes 6291464 | tf_op jit(solution)/shard_map/ppermute | solution.py:51
  898.7 60.9 %copy-start.7 = (bf16[512,2048]{1,0:T(8,128)(2,1)}, bf16[512,2048]{1,0:T(8,128)(2,1)S(1)}, u32[]{:S(2)}) copy-start(bf16[512,2048]{1,0:T(8,128)(2,1)S(1)} %collective-permute-done.1) | copy-start | bytes 6291460
  899.3 51.3 %collective-permute-start.2 = (bf16[1024,2048]{1,0:T(8,128)(2,1)S(1)}, bf16[1024,2048]{1,0:T(8,128)(2,1)S(1)}, u32[]{:S(2)}, u32[]{:S(2)}) collective-permute-start(bf16[1024,2048]{1,0:T(8,128)(2,1)S(1)} %pad_maximum_fusion.1), channel_id=1, source_target_pairs={{0,28},{1,29},{2,30},{3,31},{4,0},{5,1},{6,2},{7,3},{8,4},{9,5},{1... | collective-permute-start | bytes 12582920 | tf_op jit(solution)/shard_map/ppermute | solution.py:51
  950.6 11.5 copy-start.2
  955.2 220.7 %collective-permute-start.3 = (bf16[2048,2048]{1,0:T(8,128)(2,1)}, bf16[2048,2048]{1,0:T(8,128)(2,1)S(1)}, u32[]{:S(2)}, u32[]{:S(2)}) collective-permute-start(bf16[2048,2048]{1,0:T(8,128)(2,1)} %pad_maximum_fusion), channel_id=1, source_target_pairs={{0,24},{1,25},{2,26},{3,27},{4,28},{5,29},{6,30},{7,31},{8,0},{9,1... | collective-permute-start | bytes 25165832 | tf_op jit(solution)/shard_map/ppermute | solution.py:51
  1175.8 8.3 copy-start.6
  1175.8 8.3 copy-start.21
  1184.1 476.2 %collective-permute-start.4 = (bf16[4096,2048]{1,0:T(8,128)(2,1)}, bf16[4096,2048]{1,0:T(8,128)(2,1)}, u32[]{:S(2)}, u32[]{:S(2)}) collective-permute-start(bf16[4096,2048]{1,0:T(8,128)(2,1)} %get-tuple-element.44), channel_id=1, source_target_pairs={{0,16},{1,17},{2,18},{3,19},{4,20},{5,21},{6,22},{7,23},{8,24},{9,... | collective-permute-start | bytes 50331656 | tf_op jit(solution)/shard_map/ppermute | solution.py:51
  1660.2 15.6 copy-start.10
  1660.2 16.7 copy-start.8
  1674.8 3.6 copy-start.3
  (8 other events, 11.8 us)
Sparse Core Ops, SparseCore 0:
  11.0 56.6 all-gather.6
  70.7 78.3 all-gather.8
  152.0 76.8 all-gather.10
  231.6 193.3 all-gather.12
  427.8 192.9 all-gather.14
  682.1 17.8 reduce-scatter.18
  708.2 162.9 all-reduce.21
  874.0 168.9 reduce-scatter.10
  1046.0 360.9 reduce-scatter.8
  1409.8 362.1 reduce-scatter.12
  1775.1 1408.5 reduce-scatter.14
  3186.5 1410.5 reduce-scatter.16
